TPU v7x, 32 devices: a whole 2x2x4 slice. The times are simulated.
32 devices in a mesh: segment: 16 (over z, x, core), slab: 2 (over y).
Axes of the slice: x: 2, y: 2, z: 4, core: 2. Of those that a mesh axis runs over, the one named last changes fastest.
Arguments:
- fwd_in: bfloat16 [16, 2, 32, 4, 4, 128], P('segment', None, None, 'slab'), may hold values from -6 to 6
- back_out: bfloat16 [16, 2, 32, 4, 4, 128], P('segment', None, None, 'slab'), may hold values from -6 to 6
- back_grad: bfloat16 [16, 2, 32, 4, 4, 128], P('segment', None, None, 'slab'), may hold values from -6 to 6
- batch_next: bfloat16 [2, 32, 4, 4, 128], P(None, None, 'slab'), may hold values from -6 to 6
- loss_grad: bfloat16 [2, 2, 32, 4, 4, 128], P(None, None, None, 'slab'), may hold values from -6 to 6
- weights: bfloat16 [16, 2, 32, 864], P('segment'), may hold values from -0.21875 to 0.21875
Outputs:
- fwd_out: bfloat16 [16, 2, 32, 4, 4, 128], P('segment', None, None, 'slab')
- back_acts: bfloat16 [16, 2, 32, 4, 4, 128], P('segment', None, None, 'slab')
- back_grads: bfloat16 [16, 2, 32, 4, 4, 128], P('segment', None, None, 'slab')
- weight_grads: float32 [16, 2, 32, 864], P('segment', None, None, 'slab')
All inputs are finite; a program needn't handle non-finite values.
Results may differ from a plain program's by a relative error of at most 0.012.
Values may be sent and summed in bfloat16 or wider, within the bound.
A program may use at most 64 MiB of HBM per device.

v0:
```python
import functools

import jax
import jax.numpy as jnp
from jax import lax
from jax.experimental import pallas as pl
from jax.experimental.pallas import tpu as pltpu
from jax.sharding import PartitionSpec as P

MESH = pl.DeviceIdType.MESH
F, G, FT, GT = range(4)
X1, X2, O1, O2, G1, G2 = range(6)
Y1, Y2, R1, R2, E1, E2 = range(6)
PX, PH, PD, PY, PU, PE = range(6)


def sigmoid(v):
    return 1.0 / (1.0 + jnp.exp(-v))


def silu(v):
    return v / (1.0 + jnp.exp(-v))


def slope(v):
    sig = sigmoid(v)
    return sig * (1.0 + v * (1.0 - sig))


def kernel(
    dims, fwd, bout, bgrad, nxt, loss, w, fout, backs, grads, dw,
    pad, stage, second, made, nat, acc, g3, dsum, dpart, dgot,
    halo_s, halo_r, seg_s, seg_r, out_s, d_s, d_r,
):
    C, D, H, W, segs, n, scale = dims
    DH, HW = D * H, H * W
    cs = C // n
    f32, bf16 = jnp.float32, jnp.bfloat16
    seg = lax.axis_index("segment")
    slab = lax.axis_index("slab")
    has_prev, has_next = seg > 0, seg < segs - 1
    is_first, is_last = seg == 0, seg == segs - 1
    prev_seg = lax.rem(seg + segs - 1, segs)
    next_seg = lax.rem(seg + 1, segs)
    lane_no = lax.broadcasted_iota(jnp.int32, (C, W), 1)

    barrier = pltpu.get_barrier_semaphore()

    @pl.when(has_prev)
    def _():
        pl.semaphore_signal(barrier, inc=1, device_id={"segment": prev_seg}, device_id_type=MESH)

    @pl.when(has_next)
    def _():
        pl.semaphore_signal(barrier, inc=1, device_id={"segment": next_seg}, device_id_type=MESH)

    for k in range(1, n):
        pl.semaphore_signal(
            barrier, inc=1, device_id={"slab": lax.rem(slab + k, n)}, device_id_type=MESH
        )

    def lane(q, hh):
        return (q * (H + 2) + hh) * W

    zero = jnp.zeros((C, W), bf16)
    for t in range(2):
        for k in range(6):
            for q in range(D + 2):
                for hh in (0, H + 1):
                    pad[t, k, :, pl.ds(lane(q, hh), W)] = zero

    @pl.when(slab == 0)
    def _():
        for t in range(2):
            for k in range(6):
                pad[t, k, :, pl.ds(lane(0, 1), HW)] = jnp.zeros((C, HW), bf16)

    @pl.when(slab == n - 1)
    def _():
        for t in range(2):
            for k in range(6):
                pad[t, k, :, pl.ds(lane(D + 1, 1), HW)] = jnp.zeros((C, HW), bf16)

    def load_stage(slot, ref, s):
        stage[slot] = ref[s].astype(f32)

    def staged(slot, r):
        return stage[slot, pl.ds(r, C, stride=DH), :]

    for s in range(2):
        load_stage(G1 + s, bgrad, s)
        load_stage(O1 + s, bout, s)
        load_stage(X1 + s, fwd, s)

    def halo(t, k, up):
        src_q, dst_q = (D, 0) if up else (1, D + 1)
        target = lax.rem(slab + (1 if up else n - 1), n)
        return pltpu.make_async_remote_copy(
            src_ref=pad.at[t, k, :, pl.ds(lane(src_q, 1), HW)],
            dst_ref=pad.at[t, k, :, pl.ds(lane(dst_q, 1), HW)],
            send_sem=halo_s.at[t, k, up],
            recv_sem=halo_r.at[t, k, up],
            device_id={"slab": target},
            device_id_type=MESH,
        )

    def halo_start(t, k):
        @pl.when(slab < n - 1)
        def _():
            halo(t, k, 1).start()

        @pl.when(slab > 0)
        def _():
            halo(t, k, 0).start()

    def halo_arrived(t, k):
        @pl.when(slab > 0)
        def _():
            halo(t, k, 1).wait_recv()

        @pl.when(slab < n - 1)
        def _():
            halo(t, k, 0).wait_recv()

    def halo_sent(t, k):
        @pl.when(slab < n - 1)
        def _():
            halo(t, k, 1).wait_send()

        @pl.when(slab > 0)
        def _():
            halo(t, k, 0).wait_send()

    def to_next(k):
        return pltpu.make_async_remote_copy(
            src_ref=made.at[0, k], dst_ref=second.at[X1 + k],
            send_sem=seg_s.at[0, k], recv_sem=seg_r.at[0, k],
            device_id={"segment": next_seg}, device_id_type=MESH,
        )

    def to_prev(k):
        return pltpu.make_async_remote_copy(
            src_ref=made.at[0, k], dst_ref=second.at[k],
            send_sem=seg_s.at[0, k], recv_sem=seg_r.at[0, k],
            device_id={"segment": prev_seg}, device_id_type=MESH,
        )

    def out_prev(k):
        dst = backs.at[k - R1] if k < E1 else grads.at[k - E1]
        return pltpu.make_async_remote_copy(
            src_ref=nat.at[k], dst_ref=dst,
            send_sem=seg_s.at[1, k], recv_sem=seg_r.at[1, k],
            device_id={"segment": prev_seg}, device_id_type=MESH,
        )

    def own_out(k):
        return pltpu.make_async_copy(nat.at[k], fout.at[k], out_s.at[k])

    def last_act(k):
        return pltpu.make_async_copy(nat.at[k], backs.at[k], out_s.at[2 + k])

    def last_grad(k):
        return pltpu.make_async_copy(loss.at[2 + k], grads.at[k], out_s.at[4 + k])

    def put(t, k, r, value):
        d, h = divmod(r, H)
        pad[t, k, :, pl.ds(lane(d + 1, h + 1), W)] = value.astype(bf16)

    def tall(t, k, q):
        return jnp.concatenate([pad[t, k, :, pl.ds(lane(q, b), HW)] for b in range(3)], axis=0)

    def conv_local(t, k, m, slot):
        for p in range(D):
            total = None
            for a in range(3):
                if 1 <= p + a <= D:
                    part = jnp.dot(w[m, a], tall(t, k, p + a), preferred_element_type=f32)
                    total = part if total is None else total + part
            acc[slot, :, pl.ds(p * HW, HW)] = total

    def conv_finish(t, k, m, slot):
        for p in range(D):
            total = acc[slot, :, pl.ds(p * HW, HW)]
            for a in range(3):
                if not 1 <= p + a <= D:
                    total += jnp.dot(w[m, a], tall(t, k, p + a), preferred_element_type=f32)
            for h in range(H):
                y = total[:, h * W : (h + 1) * W]
                left = jnp.where(lane_no == 0, 0.0, pltpu.roll(y[:C], 1, 1))
                right = jnp.where(lane_no == W - 1, 0.0, pltpu.roll(y[2 * C :], W - 1, 1))
                yield p * H + h, y[C : 2 * C] + left + right

    def widen(j, r, v):
        at = pl.ds(r * W, W)
        g3[j, 0:C, at] = jnp.where(lane_no == W - 1, 0.0, pltpu.roll(v, W - 1, 1)).astype(bf16)
        g3[j, C : 2 * C, at] = v.astype(bf16)
        g3[j, 2 * C : 3 * C, at] = jnp.where(lane_no == 0, 0.0, pltpu.roll(v, 1, 1)).astype(bf16)

    def wgrad(t, k, j):
        total = None
        for p in range(D):
            lhs = jnp.concatenate([tall(t, k, p + a) for a in range(3)], axis=0)
            part = lax.dot_general(
                lhs, g3[j, :, pl.ds(p * HW, HW)], (((1,), (1,)), ((), ())),
                preferred_element_type=f32,
            )
            total = part if total is None else total + part
        if t == 0:
            dsum[j] = total
            return
        total += dsum[j]
        for q in range(n):
            for ab in range(9):
                dpart[j, q, ab] = total[ab * C + q * cs : ab * C + (q + 1) * cs]
        for q in range(1, n):
            share(j, q).start()

    def share(j, q):
        target = lax.rem(slab + q, n)
        return pltpu.make_async_remote_copy(
            src_ref=dpart.at[j, target], dst_ref=dgot.at[j, q],
            send_sem=d_s.at[j, q], recv_sem=d_r.at[j, q],
            device_id={"slab": target}, device_id_type=MESH,
        )

    def keep(t, k, r, value):
        held = value.astype(bf16)
        made[t, k, :, pl.ds(r * W, W)] = held
        wide = held.astype(f32)
        if t == 1:
            stage[k, pl.ds(r, C, stride=DH), :] = wide
        return wide

    def send_made(t, k):
        if t == 0:
            if k < R1:
                @pl.when(has_next)
                def _():
                    to_next(k).start()

                @pl.when(is_last)
                def _():
                    second[O1 + k] = made[0, k]
            else:
                @pl.when(has_prev)
                def _():
                    to_prev(k).start()
            return
        nat[k] = stage[k].astype(bf16)
        if k < R1:
            own_out(k).start()

            @pl.when(is_last)
            def _():
                last_act(k).start()
        else:
            @pl.when(has_prev)
            def _():
                out_prev(k).start()

    def tick(t, get, ready):
        ready(G2)
        for r in range(DH):
            put(t, PD, r, get(G2, r))
        if t == 0:
            peers = has_prev.astype(jnp.int32) + has_next.astype(jnp.int32) + n - 1
            pl.semaphore_wait(barrier, peers)
        halo_start(t, PD)
        ready(O1)
        for r in range(DH):
            put(t, PH, r, silu(get(O1, r)))
        halo_start(t, PH)
        ready(X2)
        for r in range(DH):
            put(t, PX, r, silu(get(X2, r)))
        halo_start(t, PX)
        conv_local(t, PD, GT, 0)
        conv_local(t, PH, G, 1)
        conv_local(t, PX, F, 2)
        for r in range(DH):
            widen(1, r, get(G2, r))

        ready(G1)
        halo_arrived(t, PD)
        for r, out in conv_finish(t, PD, GT, 0):
            put(t, PE, r, keep(t, E1, r, get(G1, r) + slope(get(O1, r)) * out))
        halo_start(t, PE)
        send_made(t, E1)
        ready(O2)
        halo_arrived(t, PH)
        for r, out in conv_finish(t, PH, G, 1):
            put(t, PU, r, silu(keep(t, R2, r, get(O2, r) - out)))
        halo_start(t, PU)
        send_made(t, R2)
        ready(X1)
        halo_arrived(t, PX)
        for r, out in conv_finish(t, PX, F, 2):
            put(t, PY, r, silu(keep(t, Y1, r, get(X1, r) + out)))
        halo_start(t, PY)
        send_made(t, Y1)

        conv_local(t, PE, FT, 0)
        conv_local(t, PU, F, 1)
        conv_local(t, PY, G, 2)
        wgrad(t, PH, 1)
        for r in range(DH):
            widen(0, r, made[t, E1, :, pl.ds(r * W, W)].astype(f32))

        halo_arrived(t, PE)
        for r, out in conv_finish(t, PE, FT, 0):
            v = made[t, R2, :, pl.ds(r * W, W)].astype(f32)
            keep(t, E2, r, get(G2, r) + slope(v) * out)
        send_made(t, E2)
        halo_arrived(t, PU)
        if t == 1:
            wgrad(t, PU, 0)
        for r, out in conv_finish(t, PU, F, 1):
            keep(t, R1, r, get(O1, r) - out)
        send_made(t, R1)
        halo_arrived(t, PY)
        for r, out in conv_finish(t, PY, G, 2):
            keep(t, Y2, r, get(X2, r) + out)
        send_made(t, Y2)
        if t == 0:
            wgrad(t, PU, 0)

    tick(0, staged, lambda k: None)

    @pl.when(is_first)
    def _():
        for s in range(2):
            load_stage(X1 + s, nxt, s)
            for r in range(DH):
                second[X1 + s, :, pl.ds(r * W, W)] = staged(X1 + s, r).astype(bf16)

    @pl.when(is_last)
    def _():
        for s in range(2):
            last_grad(s).start()
            load_stage(G1 + s, loss, s)
            for r in range(DH):
                second[G1 + s, :, pl.ds(r * W, W)] = staged(G1 + s, r).astype(bf16)

    def arrived(k):
        if k <= X2:
            @pl.when(has_prev)
            def _():
                to_next(k).wait_recv()
        else:
            @pl.when(has_next)
            def _():
                to_prev(k).wait_recv()

    tick(1, lambda k, r: second[k, :, pl.ds(r * W, W)].astype(f32), arrived)

    for j in (1, 0):
        for q in range(1, n):
            share(j, q).wait_recv()
        total = dpart[j, slab]
        for q in range(1, n):
            total += dgot[j, q]
        dw[j] = total * scale

    for t in range(2):
        for k in range(6):
            halo_sent(t, k)
    for j in range(2):
        for q in range(1, n):
            share(j, q).wait_send()
    for k in (Y1, Y2):
        own_out(k).wait()

    @pl.when(is_last)
    def _():
        for k in (Y1, Y2):
            last_act(k).wait()
            last_grad(k).wait()

    @pl.when(has_next)
    def _():
        for k in (Y1, Y2):
            to_next(k).wait_send()
        for k in (R1, R2, E1, E2):
            out_prev(k).wait_recv()

    @pl.when(has_prev)
    def _():
        for k in (R1, R2, E1, E2):
            to_prev(k).wait_send()
            out_prev(k).wait_send()


def local(segs, n, fwd_in, back_out, back_grad, batch_next, loss_grad, weights):
    _, _, C, D, H, W = fwd_in.shape
    rows = C * D * H
    cs = C // n
    f32, bf16 = jnp.float32, jnp.bfloat16
    scale = float(D * n * H * W) ** (-0.5)
    kern = weights[0].reshape(2, C, C, 3, 3, 3)
    straight = kern.transpose(0, 3, 5, 1, 4, 2)
    turned = jnp.flip(kern, (3, 4, 5)).transpose(0, 3, 5, 2, 4, 1)
    w = jnp.concatenate([straight, turned], axis=0).reshape(4, 3, 3 * C, 3 * C)
    vmem = pl.BlockSpec(memory_space=pltpu.VMEM)
    anywhere = pl.BlockSpec(memory_space=pl.ANY)
    pair = jax.ShapeDtypeStruct((2, rows, W), bf16)
    dma = pltpu.SemaphoreType.DMA
    fout, backs, grads, dw = pl.pallas_call(
        functools.partial(kernel, (C, D, H, W, segs, n, scale)),
        out_shape=(pair, pair, pair, jax.ShapeDtypeStruct((2, 9, cs, 3 * C), f32)),
        in_specs=[vmem] * 6,
        out_specs=(anywhere, anywhere, anywhere, vmem),
        scratch_shapes=[
            pltpu.VMEM((2, 6, C, (D + 2) * (H + 2) * W), bf16),
            pltpu.VMEM((6, rows, W), f32),
            pltpu.VMEM((6, C, D * H * W), bf16),
            pltpu.VMEM((2, 6, C, D * H * W), bf16),
            pltpu.VMEM((6, rows, W), bf16),
            pltpu.VMEM((3, 3 * C, D * H * W), f32),
            pltpu.VMEM((2, 3 * C, D * H * W), bf16),
            pltpu.VMEM((2, 9 * C, 3 * C), f32),
            pltpu.VMEM((2, n, 9, cs, 3 * C), f32),
            pltpu.VMEM((2, n, 9, cs, 3 * C), f32),
            dma((2, 6, 2)),
            dma((2, 6, 2)),
            dma((2, 6)),
            dma((2, 6)),
            dma((6,)),
            dma((2, n)),
            dma((2, n)),
        ],
        compiler_params=pltpu.CompilerParams(
            collective_id=0, has_side_effects=True, vmem_limit_bytes=48 * 2**20
        ),
        name="petra",
    )(
        fwd_in.reshape(2, rows, W),
        back_out.reshape(2, rows, W),
        back_grad.reshape(2, rows, W),
        batch_next.reshape(2, rows, W),
        loss_grad.reshape(4, rows, W),
        w,
    )
    dw = dw.reshape(2, 3, 3, cs, 3, C).transpose(0, 5, 3, 1, 2, 4).reshape(1, 2, C, cs * 27)
    shape = fwd_in.shape
    return fout.reshape(shape), backs.reshape(shape), grads.reshape(shape), dw


def solution(mesh):
    field = P("segment", None, None, "slab", None, None)
    return jax.shard_map(
        functools.partial(local, mesh.shape["segment"], mesh.shape["slab"]),
        mesh=mesh,
        in_specs=(
            field,
            field,
            field,
            P(None, None, "slab", None, None),
            P(None, None, None, "slab", None, None),
            P("segment", None, None, None),
        ),
        out_specs=(field, field, field, P("segment", None, None, "slab")),
        check_vma=False,
    )
```

profile of v0, /device:TPU:1, one launch (start us, length us, event | category | flops | bytes accessed | tf_op | source)
XLA Modules:
  0.0 32.5 jit_solution(5257637920858129411)
XLA Ops:
  0.6 1.5 %copy.13 = bf16[1,2,32,864]{2,1,3,0:T(2,128)(2,1)S(1)} copy(bf16[1,2,32,864]{3,2,1,0:T(8,128)(2,1)} %param.11) | data formatting | bytes 221184 | tf_op args[5]
  2.1 0.3 reverse_bitcast_fusion
  2.4 0.6 %copy.14 = bf16[2,32,32,3,3,3]{2,0,5,4,3,1:T(2,128)(2,1)S(1)} copy(bf16[2,32,32,3,3,3]{1,0,5,4,3,2:T(2,128)(2,1)S(1)} %bitcast.25) | data formatting | bytes 221184 | tf_op jit(solution)/shard_map/reshape;squeeze | solution.py:399
  3.1 1.1 %pad_maximum_fusion = bf16[4,3,3,32,3,32]{5,0,2,4,1,3:T(4,128)(2,1)S(1)} fusion(bf16[2,3,3,32,3,32]{5,0,2,4,1,3:T(2,128)(2,1)S(1)} %reverse_bitcast_fusion, bf16[2,3,3,32,3,32]{5,0,2,4,1,3:T(2,128)(2,1)S(1)} %bitcast.27), kind=kLoop, calls=%fused_computation | loop fusion | flops 442368 | bytes 442368 | tf_op jit(solution)/shard_map/concatenate | solution.py:402
  4.2 0.6 %copy.15 = bf16[4,3,3,32,3,32]{5,4,3,2,1,0:T(4,128)(2,1)S(1)} copy(bf16[4,3,3,32,3,32]{5,0,2,4,1,3:T(4,128)(2,1)S(1)} %pad_maximum_fusion) | data formatting | bytes 442368 | tf_op jit(solution)/shard_map/concatenate | solution.py:402
  4.9 0.0 copy-start
  4.9 0.0 copy-start.1
  4.9 0.0 copy-start.2
  4.9 0.0 copy-start.3
  4.9 0.0 copy-start.4
  4.9 0.6 %reshape.46.w = bf16[4,3,96,96]{3,2,1,0:T(8,128)(2,1)S(1)} reshape(bf16[4,3,3,32,3,32]{5,4,3,2,1,0:T(4,128)(2,1)S(1)} %copy.15) | data formatting | bytes 442368 | tf_op jit(solution)/shard_map/reshape | solution.py:402
  5.5 0.3 copy-done
  5.8 0.0 copy-done.1
  5.9 0.1 copy-done.2
  5.9 0.1 copy-done.3
  6.0 0.0 copy-done.4
  6.0 23.0 %petra.1 = (bf16[2,256,128]{2,1,0:T(8,128)(2,1)S(1)}, bf16[2,256,128]{2,1,0:T(8,128)(2,1)S(1)}, bf16[2,256,128]{2,1,0:T(8,128)(2,1)S(1)}, f32[2,9,16,96]{3,2,1,0:T(8,128)S(1)}) custom-call(bf16[2,256,128]{2,1,0:T(8,128)(2,1)S(1)} %bitcast.17, bf16[2,256,128]{2,1,0:T(8,128)(2,1)S(1)} %bitcast.18, bf16[2,256,128]{2,1,0:T(8,128)(2,1)S(1)} %bitcast.19, ...), custom_call_target="tpu_custom_call" | custom-call | tf_op jit(solution)/shard_map/petra/pallas_call | solution.py:407
  29.1 0.2 reshape.50
  29.3 0.3 %copy.16 = f32[2,32,16,3,3,3]{1,0,5,4,3,2:T(2,128)S(1)} copy(f32[2,32,16,3,3,3]{1,5,2,4,3,0:T(4,128)S(1)} %bitcast.26) | data formatting | bytes 221184 | tf_op jit(solution)/shard_map/transpose | solution.py:443
  29.7 0.8 %copy.17 = f32[1,2,32,432]{3,2,1,0:T(8,128)} copy(f32[1,2,32,432]{2,1,3,0:T(2,128)S(1)} %bitcast.28) | data formatting | bytes 221184
  30.5 0.7 %copy.21 = bf16[1,2,32,2,4,128]{5,4,3,2,1,0:T(4,128)(2,1)} copy(bf16[1,2,32,2,4,128]{5,4,3,2,1,0:T(4,128)(2,1)S(1)} %bitcast.23) | data formatting | bytes 262144
  31.2 0.7 %copy.22 = bf16[1,2,32,2,4,128]{5,4,3,2,1,0:T(4,128)(2,1)} copy(bf16[1,2,32,2,4,128]{5,4,3,2,1,0:T(4,128)(2,1)S(1)} %bitcast.22) | data formatting | bytes 262144
  31.8 0.7 %copy.23 = bf16[1,2,32,2,4,128]{5,4,3,2,1,0:T(4,128)(2,1)} copy(bf16[1,2,32,2,4,128]{5,4,3,2,1,0:T(4,128)(2,1)S(1)} %bitcast.21) | data formatting | bytes 262144
Async XLA Ops:
  4.9 1.0 %copy-start = (bf16[2,2,32,2,4,128]{5,4,3,2,1,0:T(4,128)(2,1)S(1)}, bf16[2,2,32,2,4,128]{5,4,3,2,1,0:T(4,128)(2,1)}, u32[]{:S(2)}) copy-start(bf16[2,2,32,2,4,128]{5,4,3,2,1,0:T(4,128)(2,1)} %param.10) | copy-start | bytes 786436
  4.9 1.0 %copy-start.1 = (bf16[1,2,32,2,4,128]{5,4,3,2,1,0:T(4,128)(2,1)S(1)}, bf16[1,2,32,2,4,128]{5,4,3,2,1,0:T(4,128)(2,1)}, u32[]{:S(2)}) copy-start(bf16[1,2,32,2,4,128]{5,4,3,2,1,0:T(4,128)(2,1)} %param.6) | copy-start | bytes 393220
  4.9 1.0 %copy-start.2 = (bf16[1,2,32,2,4,128]{5,4,3,2,1,0:T(4,128)(2,1)S(1)}, bf16[1,2,32,2,4,128]{5,4,3,2,1,0:T(4,128)(2,1)}, u32[]{:S(2)}) copy-start(bf16[1,2,32,2,4,128]{5,4,3,2,1,0:T(4,128)(2,1)} %param.7) | copy-start | bytes 393220
  4.9 1.1 %copy-start.3 = (bf16[1,2,32,2,4,128]{5,4,3,2,1,0:T(4,128)(2,1)S(1)}, bf16[1,2,32,2,4,128]{5,4,3,2,1,0:T(4,128)(2,1)}, u32[]{:S(2)}) copy-start(bf16[1,2,32,2,4,128]{5,4,3,2,1,0:T(4,128)(2,1)} %param.8) | copy-start | bytes 393220
  4.9 1.1 %copy-start.4 = (bf16[2,32,2,4,128]{4,3,2,1,0:T(4,128)(2,1)S(1)}, bf16[2,32,2,4,128]{4,3,2,1,0:T(4,128)(2,1)}, u32[]{:S(2)}) copy-start(bf16[2,32,2,4,128]{4,3,2,1,0:T(4,128)(2,1)} %param.9) | copy-start | bytes 393220
where the time goes:
time: 32.7 us; the launch traced here: 32.5 us
  Pallas kernels  23 us (70%)
  local copies, waits for them, and re-layouts  7.56 us (23%)
  other arithmetic  1.14 us (3%)
  between operations  0.74 us (2%)
    pallas_call x1, Pallas kernels, local(): pl.pallas_call(functools.partial(kernel, (C, D, H, W, segs, n, scale)), o...  23 us
    unnamed x15, local copies, waits for them, and re-layouts  4.85 us
    concatenate x1, other arithmetic, local(): w = jnp.concatenate([straight, turned], axis=0).reshape(4, 3, 3 * C, 3 * C)  1.14 us

commit v1 on v0

--- a/solution.py
+++ b/solution.py
@@ -28,13 +28,14 @@
 
 
 def kernel(
-    dims, fwd, bout, bgrad, nxt, loss, w, fout, backs, grads, dw,
-    pad, stage, second, made, nat, acc, g3, dsum, dpart, dgot,
-    halo_s, halo_r, seg_s, seg_r, out_s, d_s, d_r,
+    dims, fwd_hbm, bout_hbm, bgrad_hbm, nxt_hbm, loss_hbm, kern_hbm, fout, backs, grads, dw,
+    fwd, bout, bgrad, nxt, loss, kern, kt, w, dt, pad, stage, second, made, nat, acc, g3, dsum, dpart, dgot,
+    halo_s, halo_r, seg_s, seg_r, out_s, d_s, d_r, in_s,
 ):
     C, D, H, W, segs, n, scale = dims
     DH, HW = D * H, H * W
     cs = C // n
+    LW = pl.cdiv(3 * C, 128) * 128
     f32, bf16 = jnp.float32, jnp.bfloat16
     seg = lax.axis_index("segment")
     slab = lax.axis_index("slab")
@@ -44,6 +45,18 @@
     next_seg = lax.rem(seg + 1, segs)
     lane_no = lax.broadcasted_iota(jnp.int32, (C, W), 1)
 
+    fetches = [
+        pltpu.make_async_copy(src, dst, in_s.at[i])
+        for i, (src, dst) in enumerate(
+            [
+                (bgrad_hbm, bgrad), (bout_hbm, bout), (fwd_hbm, fwd),
+                (kern_hbm, kern), (nxt_hbm, nxt), (loss_hbm, loss),
+            ]
+        )
+    ]
+    for fetch in fetches:
+        fetch.start()
+
     barrier = pltpu.get_barrier_semaphore()
 
     @pl.when(has_prev)
@@ -87,10 +100,33 @@
     def staged(slot, r):
         return stage[slot, pl.ds(r, C, stride=DH), :]
 
-    for s in range(2):
-        load_stage(G1 + s, bgrad, s)
-        load_stage(O1 + s, bout, s)
-        load_stage(X1 + s, fwd, s)
+    def prepare_weights():
+        fetches[3].wait()
+        wide = kern[...].astype(f32)
+        kt[...] = jnp.concatenate([wide, jnp.zeros((LW - 2 * C, 27 * C), f32)], axis=0).T
+
+        def tap(t):
+            return kt[pl.ds(t, C, stride=27), :]
+
+        for a in range(3):
+            for c in range(3):
+                block = jnp.concatenate([tap(9 * a + 3 * b + c) for b in range(3)], axis=0).T
+                for f in range(2):
+                    w[F + f, a, c * C : (c + 1) * C, :] = block[f * C : (f + 1) * C].astype(bf16)
+                for f in range(2):
+                    turned = jnp.concatenate(
+                        [
+                            tap(9 * (2 - a) + 3 * (2 - b) + 2 - c)[:, f * C : (f + 1) * C]
+                            for b in range(3)
+                        ],
+                        axis=1,
+                    )
+                    w[FT + f, a, c * C : (c + 1) * C, :] = turned.astype(bf16)
+
+    def load_pair(i, slot, ref):
+        fetches[i].wait()
+        for s in range(2):
+            load_stage(slot + s, ref, s)
 
     def halo(t, k, up):
         src_q, dst_q = (D, 0) if up else (1, D + 1)
@@ -209,6 +245,7 @@
             dsum[j] = total
             return
         total += dsum[j]
+        total = jnp.concatenate([total, jnp.zeros((9 * C, LW - 3 * C), f32)], axis=1)
         for q in range(n):
             for ab in range(9):
                 dpart[j, q, ab] = total[ab * C + q * cs : ab * C + (q + 1) * cs]
@@ -259,6 +296,8 @@
                 out_prev(k).start()
 
     def tick(t, get, ready):
+        if t == 0:
+            load_pair(0, G1, bgrad)
         ready(G2)
         for r in range(DH):
             put(t, PD, r, get(G2, r))
@@ -266,14 +305,20 @@
             peers = has_prev.astype(jnp.int32) + has_next.astype(jnp.int32) + n - 1
             pl.semaphore_wait(barrier, peers)
         halo_start(t, PD)
+        if t == 0:
+            load_pair(1, O1, bout)
         ready(O1)
         for r in range(DH):
             put(t, PH, r, silu(get(O1, r)))
         halo_start(t, PH)
+        if t == 0:
+            load_pair(2, X1, fwd)
         ready(X2)
         for r in range(DH):
             put(t, PX, r, silu(get(X2, r)))
         halo_start(t, PX)
+        if t == 0:
+            prepare_weights()
         conv_local(t, PD, GT, 0)
         conv_local(t, PH, G, 1)
         conv_local(t, PX, F, 2)
@@ -326,6 +371,9 @@
 
     tick(0, staged, lambda k: None)
 
+    fetches[4].wait()
+    fetches[5].wait()
+
     @pl.when(is_first)
     def _():
         for s in range(2):
@@ -359,7 +407,12 @@
         total = dpart[j, slab]
         for q in range(1, n):
             total += dgot[j, q]
-        dw[j] = total * scale
+        total *= scale
+        for ab in range(9):
+            for c in range(3):
+                tap = total[ab] if c == 0 else pltpu.roll(total[ab], LW - c * C, 1)
+                dt[j, pl.ds(3 * ab + c, cs, stride=27), :] = tap
+        dw[j] = dt[j].T[:C]
 
     for t in range(2):
         for k in range(6):
@@ -390,26 +443,47 @@
             out_prev(k).wait_send()
 
 
+def write_out(*refs):
+    srcs, dsts, tiles, sems = refs[:4], refs[4:8], refs[8:12], refs[12]
+    reads = [pltpu.make_async_copy(a, b, sems.at[0, i]) for i, (a, b) in enumerate(zip(srcs, tiles))]
+    writes = [pltpu.make_async_copy(a, b, sems.at[1, i]) for i, (a, b) in enumerate(zip(tiles, dsts))]
+    for read in reads:
+        read.start()
+    for read, write in zip(reads, writes):
+        read.wait()
+        write.start()
+    for write in writes:
+        write.wait()
+
+
 def local(segs, n, fwd_in, back_out, back_grad, batch_next, loss_grad, weights):
     _, _, C, D, H, W = fwd_in.shape
     rows = C * D * H
     cs = C // n
     f32, bf16 = jnp.float32, jnp.bfloat16
     scale = float(D * n * H * W) ** (-0.5)
-    kern = weights[0].reshape(2, C, C, 3, 3, 3)
-    straight = kern.transpose(0, 3, 5, 1, 4, 2)
-    turned = jnp.flip(kern, (3, 4, 5)).transpose(0, 3, 5, 2, 4, 1)
-    w = jnp.concatenate([straight, turned], axis=0).reshape(4, 3, 3 * C, 3 * C)
     vmem = pl.BlockSpec(memory_space=pltpu.VMEM)
+    hbm = pl.BlockSpec(memory_space=pltpu.HBM)
+    wide = pl.cdiv(3 * C, 128) * 128
     anywhere = pl.BlockSpec(memory_space=pl.ANY)
     pair = jax.ShapeDtypeStruct((2, rows, W), bf16)
+    share = jax.ShapeDtypeStruct((2, C, 27 * cs), f32)
     dma = pltpu.SemaphoreType.DMA
     fout, backs, grads, dw = pl.pallas_call(
         functools.partial(kernel, (C, D, H, W, segs, n, scale)),
-        out_shape=(pair, pair, pair, jax.ShapeDtypeStruct((2, 9, cs, 3 * C), f32)),
-        in_specs=[vmem] * 6,
+        out_shape=(pair, pair, pair, share),
+        in_specs=[hbm] * 6,
         out_specs=(anywhere, anywhere, anywhere, vmem),
         scratch_shapes=[
+            pltpu.VMEM((2, rows, W), bf16),
+            pltpu.VMEM((2, rows, W), bf16),
+            pltpu.VMEM((2, rows, W), bf16),
+            pltpu.VMEM((2, rows, W), bf16),
+            pltpu.VMEM((4, rows, W), bf16),
+            pltpu.VMEM((2 * C, 27 * C), bf16),
+            pltpu.VMEM((27 * C, wide), f32),
+            pltpu.VMEM((4, 3, 3 * C, 3 * C), bf16),
+            pltpu.VMEM((2, 27 * cs, wide), f32),
             pltpu.VMEM((2, 6, C, (D + 2) * (H + 2) * W), bf16),
             pltpu.VMEM((6, rows, W), f32),
             pltpu.VMEM((6, C, D * H * W), bf16),
@@ -418,8 +492,8 @@
             pltpu.VMEM((3, 3 * C, D * H * W), f32),
             pltpu.VMEM((2, 3 * C, D * H * W), bf16),
             pltpu.VMEM((2, 9 * C, 3 * C), f32),
-            pltpu.VMEM((2, n, 9, cs, 3 * C), f32),
-            pltpu.VMEM((2, n, 9, cs, 3 * C), f32),
+            pltpu.VMEM((2, n, 9, cs, wide), f32),
+            pltpu.VMEM((2, n, 9, cs, wide), f32),
             dma((2, 6, 2)),
             dma((2, 6, 2)),
             dma((2, 6)),
@@ -427,9 +501,10 @@
             dma((6,)),
             dma((2, n)),
             dma((2, n)),
+            dma((6,)),
         ],
         compiler_params=pltpu.CompilerParams(
-            collective_id=0, has_side_effects=True, vmem_limit_bytes=48 * 2**20
+            collective_id=0, has_side_effects=True, vmem_limit_bytes=67043328
         ),
         name="petra",
     )(
@@ -438,11 +513,20 @@
         back_grad.reshape(2, rows, W),
         batch_next.reshape(2, rows, W),
         loss_grad.reshape(4, rows, W),
-        w,
+        weights.reshape(2 * C, 27 * C),
     )
-    dw = dw.reshape(2, 3, 3, cs, 3, C).transpose(0, 5, 3, 1, 2, 4).reshape(1, 2, C, cs * 27)
+    fout, backs, grads, dw = pl.pallas_call(
+        write_out,
+        out_shape=(pair, pair, pair, share),
+        in_specs=[hbm] * 4,
+        out_specs=(hbm,) * 4,
+        scratch_shapes=[pltpu.VMEM(x.shape, x.dtype) for x in (pair, pair, pair, share)]
+        + [dma((2, 4))],
+        compiler_params=pltpu.CompilerParams(vmem_limit_bytes=67043328),
+        name="write_out",
+    )(fout, backs, grads, dw)
     shape = fwd_in.shape
-    return fout.reshape(shape), backs.reshape(shape), grads.reshape(shape), dw
+    return fout.reshape(shape), backs.reshape(shape), grads.reshape(shape), dw[None]
 
 
 def solution(mesh):

time: 32.7 us -> 26.8 us (0.82)
  local copies, waits for them, and re-layouts: 7.56 us -> 0 us
  Pallas kernels: 23 us -> 25.8 us
  other arithmetic: 1.14 us -> 0 us
    unnamed x15 -> x0, local copies, waits for them, and re-layouts: 4.85 us -> none
    pallas_call x0 -> x1, Pallas kernels: none -> 1.82 us  [local(): pl.pallas_call(write_out, out_shape=(pair, pair, pair, share), in_specs=[...]
    concatenate x1 -> x0, other arithmetic: 1.14 us -> none  [local(): w = jnp.concatenate([straight, turned], axis=0).reshape(4, 3, 3 * C, 3 * C)]
    pallas_call x1, Pallas kernels: 23 us -> 23.9 us  [local(): pl.pallas_call(functools.partial(kernel, (C, D, H, W, segs, n, scale)), o...]
    reshape x2 -> x0, local copies, waits for them, and re-layouts: 0.81 us -> none  [the longest x1 0.56 us: local(): w = jnp.concatenate([straight, turned], axis=0).reshape(4, 3, 3 * C, 3 * C)]
    transpose x2 -> x0, local copies, waits for them, and re-layouts: 0.65 us -> none  [the longest x1 0.34 us: local(): dw.reshape(2, 3, 3, cs, 3, C).transpose(0, 5, 3, 1, 2, 4)]
    another operation x1 -> x0, local copies, waits for them, and re-layouts: 0.63 us -> none  [local(): kern = weights[0].reshape(2, C, C, 3, 3, 3)]
    concatenate x1 -> x0, local copies, waits for them, and re-layouts: 0.62 us -> none  [local(): w = jnp.concatenate([straight, turned], axis=0).reshape(4, 3, 3 * C, 3 * C)]
where the time goes in v1:
time: 26.8 us; the launch traced here: 26.4 us
  Pallas kernels  25.8 us (96%)
  between operations  0.64 us (2%)
    pallas_call x1, Pallas kernels, local(): pl.pallas_call(functools.partial(kernel, (C, D, H, W, segs, n, scale)), o...  23.9 us
    pallas_call x1, Pallas kernels, local(): pl.pallas_call(write_out, out_shape=(pair, pair, pair, share), in_specs=[...  1.82 us

profile of v1, /device:TPU:1, one launch (start us, length us, event | category | flops | bytes accessed | tf_op | source)
XLA Modules:
  0.0 26.4 jit_solution(4439028943779074650)
XLA Ops:
  0.6 23.9 %petra.1 = (bf16[2,256,128]{2,1,0:T(8,128)(2,1)}, bf16[2,256,128]{2,1,0:T(8,128)(2,1)}, bf16[2,256,128]{2,1,0:T(8,128)(2,1)}, f32[2,32,432]{2,1,0:T(8,128)}) custom-call(bf16[2,256,128]{2,1,0:T(8,128)(2,1)} %bitcast.11, bf16[2,256,128]{2,1,0:T(8,128)(2,1)} %bitcast.12, bf16[2,256,128]{2,1,0:T(8,128)(2,1)} %bitcast.13, bf16[2,256,128]{2,1,0:T(8,128)(2,1)} %bitcast.14, ...), custom_call_target="tpu_custom_call" | custom-call | tf_op jit(solution)/shard_map/petra/pallas_call | solution.py:472
  24.6 1.8 %write_out.1 = (bf16[2,256,128]{2,1,0:T(8,128)(2,1)}, bf16[2,256,128]{2,1,0:T(8,128)(2,1)}, bf16[2,256,128]{2,1,0:T(8,128)(2,1)}, f32[2,32,432]{2,1,0:T(8,128)}) custom-call(bf16[2,256,128]{2,1,0:T(8,128)(2,1)} %get-tuple-element.12.refs_0_, bf16[2,256,128]{2,1,0:T(8,128)(2,1)} %get-tuple-element.13.refs_1_, bf16[2,256,128]{2,1,0:T(8,128)(2,1)} %get-tuple-element.14.refs_2_, ...), custom_call_target="tpu_custom_call" | custom-call | tf_op jit(solution)/shard_map/write_out/pallas_call | solution.py:518

commit v2 on v1

--- a/solution.py
+++ b/solution.py
@@ -30,7 +30,7 @@
 def kernel(
     dims, fwd_hbm, bout_hbm, bgrad_hbm, nxt_hbm, loss_hbm, kern_hbm, fout, backs, grads, dw,
     fwd, bout, bgrad, nxt, loss, kern, kt, w, dt, pad, stage, second, made, nat, acc, g3, dsum, dpart, dgot,
-    halo_s, halo_r, seg_s, seg_r, out_s, d_s, d_r, in_s,
+    halo_s, halo_r, seg_s, seg_r, out_s, d_s, d_r, in_s, edge, diag_s,
 ):
     C, D, H, W, segs, n, scale = dims
     DH, HW = D * H, H * W
@@ -59,13 +59,23 @@
 
     barrier = pltpu.get_barrier_semaphore()
 
-    @pl.when(has_prev)
-    def _():
-        pl.semaphore_signal(barrier, inc=1, device_id={"segment": prev_seg}, device_id_type=MESH)
-
-    @pl.when(has_next)
-    def _():
-        pl.semaphore_signal(barrier, inc=1, device_id={"segment": next_seg}, device_id_type=MESH)
+    up_slab, down_slab = lax.rem(slab + 1, n), lax.rem(slab + n - 1, n)
+    has_up, has_down = slab < n - 1, slab > 0
+
+    for there, target in ((has_prev, prev_seg), (has_next, next_seg)):
+        @pl.when(there)
+        def _():
+            pl.semaphore_signal(
+                barrier, inc=1, device_id={"segment": target}, device_id_type=MESH
+            )
+
+        for side, beside in ((has_up, up_slab), (has_down, down_slab)):
+            @pl.when(there & side)
+            def _():
+                pl.semaphore_signal(
+                    barrier, inc=1, device_id={"segment": target, "slab": beside},
+                    device_id_type=MESH,
+                )
 
     for k in range(1, n):
         pl.semaphore_signal(
@@ -140,14 +150,41 @@
             device_id_type=MESH,
         )
 
+    def exchanged(t, k):
+        if t == 0 or k >= PY:
+            return seg >= 0
+        return is_first if k == PX else is_last
+
     def halo_start(t, k):
-        @pl.when(slab < n - 1)
+        @pl.when(exchanged(t, k) & has_up)
         def _():
             halo(t, k, 1).start()
 
-        @pl.when(slab > 0)
+        @pl.when(exchanged(t, k) & has_down)
         def _():
             halo(t, k, 0).start()
+
+    def diagonal(k, up):
+        src = made.at[0, E2] if k == PD else edge.at[0 if k == PH else 1]
+        plane, dst_q = (D - 1, 0) if up else (0, D + 1)
+        return pltpu.make_async_remote_copy(
+            src_ref=src.at[:, pl.ds(plane * HW, HW)],
+            dst_ref=pad.at[1, k, :, pl.ds(lane(dst_q, 1), HW)],
+            send_sem=diag_s.at[k, up],
+            recv_sem=halo_r.at[1, k, up],
+            device_id={
+                "segment": next_seg if k == PX else prev_seg,
+                "slab": up_slab if up else down_slab,
+            },
+            device_id_type=MESH,
+        )
+
+    def each_diagonal(k, act):
+        there = has_next if k == PX else has_prev
+        for up, side in ((1, has_up), (0, has_down)):
+            @pl.when(there & side)
+            def _():
+                act(diagonal(k, up))
 
     def halo_arrived(t, k):
         @pl.when(slab > 0)
@@ -159,11 +196,11 @@
             halo(t, k, 0).wait_recv()
 
     def halo_sent(t, k):
-        @pl.when(slab < n - 1)
+        @pl.when(exchanged(t, k) & has_up)
         def _():
             halo(t, k, 1).wait_send()
 
-        @pl.when(slab > 0)
+        @pl.when(exchanged(t, k) & has_down)
         def _():
             halo(t, k, 0).wait_send()
 
@@ -302,7 +339,9 @@
         for r in range(DH):
             put(t, PD, r, get(G2, r))
         if t == 0:
-            peers = has_prev.astype(jnp.int32) + has_next.astype(jnp.int32) + n - 1
+            ends = has_prev.astype(jnp.int32) + has_next.astype(jnp.int32)
+            sides = has_up.astype(jnp.int32) + has_down.astype(jnp.int32)
+            peers = ends * (1 + sides) + n - 1
             pl.semaphore_wait(barrier, peers)
         halo_start(t, PD)
         if t == 0:
@@ -355,16 +394,26 @@
         for r, out in conv_finish(t, PE, FT, 0):
             v = made[t, R2, :, pl.ds(r * W, W)].astype(f32)
             keep(t, E2, r, get(G2, r) + slope(v) * out)
+        if t == 0:
+            each_diagonal(PD, lambda copy: copy.start())
         send_made(t, E2)
         halo_arrived(t, PU)
         if t == 1:
             wgrad(t, PU, 0)
         for r, out in conv_finish(t, PU, F, 1):
-            keep(t, R1, r, get(O1, r) - out)
+            wide = keep(t, R1, r, get(O1, r) - out)
+            if t == 0:
+                edge[0, :, pl.ds(r * W, W)] = silu(wide).astype(bf16)
+        if t == 0:
+            each_diagonal(PH, lambda copy: copy.start())
         send_made(t, R1)
         halo_arrived(t, PY)
         for r, out in conv_finish(t, PY, G, 2):
-            keep(t, Y2, r, get(X2, r) + out)
+            wide = keep(t, Y2, r, get(X2, r) + out)
+            if t == 0:
+                edge[1, :, pl.ds(r * W, W)] = silu(wide).astype(bf16)
+        if t == 0:
+            each_diagonal(PX, lambda copy: copy.start())
         send_made(t, Y2)
         if t == 0:
             wgrad(t, PU, 0)
@@ -417,6 +466,8 @@
     for t in range(2):
         for k in range(6):
             halo_sent(t, k)
+    for k in (PD, PH, PX):
+        each_diagonal(k, lambda copy: copy.wait_send())
     for j in range(2):
         for q in range(1, n):
             share(j, q).wait_send()
@@ -502,6 +553,8 @@
             dma((2, n)),
             dma((2, n)),
             dma((6,)),
+            pltpu.VMEM((2, C, D * H * W), bf16),
+            dma((3, 2)),
         ],
         compiler_params=pltpu.CompilerParams(
             collective_id=0, has_side_effects=True, vmem_limit_bytes=67043328

time: 26.8 us -> 27.8 us (1.037)
  Pallas kernels: 25.8 us -> 27 us
    pallas_call x1, Pallas kernels: 23.9 us -> 25.2 us  [local(): pl.pallas_call(functools.partial(kernel, (C, D, H, W, segs, n, scale)), o...]
where the time goes in v2:
time: 27.8 us; the launch traced here: 27.7 us
  Pallas kernels  27 us (97%)
  between operations  0.64 us (2%)
    pallas_call x1, Pallas kernels, local(): pl.pallas_call(functools.partial(kernel, (C, D, H, W, segs, n, scale)), o...  25.2 us
    pallas_call x1, Pallas kernels, local(): pl.pallas_call(write_out, out_shape=(pair, pair, pair, share), in_specs=[...  1.82 us

profile of v2, /device:TPU:1, one launch (start us, length us, event | category | flops | bytes accessed | tf_op | source)
XLA Modules:
  0.0 27.7 jit_solution(9823315116744541388)
XLA Ops:
  0.6 25.2 %petra.1 = (bf16[2,256,128]{2,1,0:T(8,128)(2,1)}, bf16[2,256,128]{2,1,0:T(8,128)(2,1)}, bf16[2,256,128]{2,1,0:T(8,128)(2,1)}, f32[2,32,432]{2,1,0:T(8,128)}) custom-call(bf16[2,256,128]{2,1,0:T(8,128)(2,1)} %bitcast.11, bf16[2,256,128]{2,1,0:T(8,128)(2,1)} %bitcast.12, bf16[2,256,128]{2,1,0:T(8,128)(2,1)} %bitcast.13, bf16[2,256,128]{2,1,0:T(8,128)(2,1)} %bitcast.14, ...), custom_call_target="tpu_custom_call" | custom-call | tf_op jit(solution)/shard_map/petra/pallas_call | solution.py:523
  25.8 1.8 %write_out.1 = (bf16[2,256,128]{2,1,0:T(8,128)(2,1)}, bf16[2,256,128]{2,1,0:T(8,128)(2,1)}, bf16[2,256,128]{2,1,0:T(8,128)(2,1)}, f32[2,32,432]{2,1,0:T(8,128)}) custom-call(bf16[2,256,128]{2,1,0:T(8,128)(2,1)} %get-tuple-element.12.refs_0_, bf16[2,256,128]{2,1,0:T(8,128)(2,1)} %get-tuple-element.13.refs_1_, bf16[2,256,128]{2,1,0:T(8,128)(2,1)} %get-tuple-element.14.refs_2_, ...), custom_call_target="tpu_custom_call" | custom-call | tf_op jit(solution)/shard_map/write_out/pallas_call | solution.py:571
